TPU v7x, 32 devices: a whole 2x2x4 slice. The times are simulated.
32 devices in a mesh: rows: 16 (over z, y, x), cols: 2 (over core).
Axes of the slice: x: 2, y: 2, z: 4, core: 2. Of those that a mesh axis runs over, the one named last changes fastest.
Arguments:
- iterate: bfloat16 [24576, 512], P('rows', 'cols'), may hold values from -256 to 256, as said below
- residual: bfloat16 [24576, 512], P('rows', 'cols'), may hold values from -256 to 256, as said below
- leaf_offset: bfloat16 [24576, 768], P('rows', 'cols'), may hold values from -0.109375 to 0.109375
- bases_v: bfloat16 [5, 24576, 256], P(None, 'rows', 'cols'), may hold values from -1 to 1, as said below
- bases_u: bfloat16 [5, 24576, 256], P(None, 'rows', 'cols'), may hold values from -0.1875 to 0.1875
- estimate: float32 [512], P('cols'), may hold values from -1 to 1
Outputs:
- updated: float32 [24576, 512], P('rows', 'cols')
- functional: float32 [512], P('cols')
Inputs may be any that keep to these rules, and one draw needn't show every extreme that they name: Entries of the iterate, real valued. Entries of the residual, real valued. `bases_v`: real valued basis entries.
All inputs are finite; a program needn't handle non-finite values.
Results may differ from a plain program's by a relative error of at most 0.0085.
Values may be sent and summed in bfloat16 or wider, within the bound.
A program may use at most 64 MiB of HBM per device.

v0:
```python
import jax
import jax.numpy as jnp
from jax import lax
from jax.sharding import PartitionSpec as P

epsilon = 1e-06


def partner(value, axis, stride):
    mask = 2**stride
    pairs = [(source, source ^ mask) for source in range(lax.axis_size(axis))]
    return lax.ppermute(value, axis, pairs)


def group_total(partial_value, bit_count):
    for bit_number in range(bit_count):
        partial_value = partial_value + partner(partial_value, "rows", bit_number)
    return partial_value


def per_device(iterate, residual, leaf_offset, bases_v, bases_u, estimate):
    rows_here, vecs_here = residual.shape
    leaf_rows = rows_here // 2
    levels = lax.axis_size("rows").bit_length() - 1
    residual_blocks = residual.reshape(2, leaf_rows, vecs_here)
    leaf_segment = lax.all_gather(leaf_offset, "cols", axis=1, tiled=True)
    blocks = leaf_segment.reshape(2, leaf_rows, leaf_segment.shape[1])
    leaf_sums = jnp.einsum(
        "kij,kjc->kic", blocks, residual_blocks, preferred_element_type=jnp.float32
    )
    current = residual.astype(jnp.float32) + leaf_sums.reshape(rows_here, vecs_here)
    for level_index in range(levels, -1, -1):
        rounded = current.astype(jnp.bfloat16)
        coefficients = lax.dot_general(
            lax.all_gather(bases_v[level_index], "cols", axis=1, tiled=True),
            rounded,
            (((0,), (0,)), ((), ())),
            preferred_element_type=jnp.float32,
        )
        coefficients = group_total(coefficients, levels - level_index)
        narrow = coefficients.astype(jnp.bfloat16)
        correction = jnp.dot(
            lax.all_gather(bases_u[level_index], "cols", axis=1, tiled=True),
            narrow,
            preferred_element_type=jnp.float32,
        )
        current = current - correction
    updated = iterate.astype(jnp.float32) - current
    numerator_local = jnp.sum(updated * residual.astype(jnp.float32), axis=0)
    denominator_local = jnp.sum(updated * updated, axis=0)
    numerator, denominator = lax.psum((numerator_local, denominator_local), "rows")
    functional = estimate + numerator / (denominator + epsilon)
    return (updated, functional)


def solution(mesh):
    return jax.shard_map(
        per_device,
        mesh=mesh,
        in_specs=(
            P("rows", "cols"),
            P("rows", "cols"),
            P("rows", "cols"),
            P(None, "rows", "cols"),
            P(None, "rows", "cols"),
            P("cols"),
        ),
        out_specs=(P("rows", "cols"), P("cols")),
        check_vma=False,
    )
```

profile of v0, /device:TPU:0, one launch (start us, length us, event | category | flops | bytes accessed | tf_op | source)
XLA Modules:
  0.0 166.4 jit_solution(5880570647379999670)
XLA Ops:
  7.2 0.7 all-gather.12.cloned.1.call-update
  7.9 0.4 copy-done
  8.6 0.4 copy-done.2
  9.0 1.2 fusion.26
  10.2 2.6 %all-gather.1 = bf16[1,1536,256]{2,1,0:T(8,128)(2,1)} all-gather(bf16[1,1536,128]{2,1,0:T(8,128)(2,1)S(1)} %get-tuple-element.16), channel_id=3, replica_groups=mesh['rows'=16,'cols'=2] {'cols'}, dimensions={2}, use_global_device_ids=true | all-gather | bytes 1179648 | tf_op jit(solution)/shard_map/all_gather | solution.py:43
  12.7 1.1 fusion.25
  13.8 2.5 %all-gather = bf16[1,1536,256]{2,1,0:T(8,128)(2,1)} all-gather(bf16[1,1536,128]{2,1,0:T(8,128)(2,1)S(1)} %get-tuple-element.11), channel_id=2, replica_groups=mesh['rows'=16,'cols'=2] {'cols'}, dimensions={2}, use_global_device_ids=true | all-gather | bytes 1179648 | tf_op jit(solution)/shard_map/all_gather | solution.py:35
  16.3 2.5 %all-gather.2 = bf16[1,1536,256]{2,1,0:T(8,128)(2,1)} all-gather(bf16[1,1536,128]{2,1,0:T(8,128)(2,1)S(1)} %get-tuple-element.10), channel_id=4, replica_groups=mesh['rows'=16,'cols'=2] {'cols'}, dimensions={2}, use_global_device_ids=true | all-gather | bytes 1179648 | tf_op jit(solution)/shard_map/all_gather | solution.py:35
  18.8 4.4 %all-gather.12.cloned.1.call-done = bf16[1536,768]{1,0:T(8,128)(2,1)} async-done(((bf16[1536,384]{1,0:T(8,128)(2,1)}), bf16[1536,768]{1,0:T(8,128)(2,1)}) %all-gather.12.cloned.1.call-update) | async-done | bytes 2359312 | tf_op jit(solution)/shard_map/all_gather | solution.py:26
  23.2 2.4 %fusion.27 = f32[2,768,256]{2,1,0:T(8,128)S(1)} fusion(bf16[2,768,768]{2,1,0:T(8,128)(2,1)} %bitcast.70, bf16[2,768,256]{2,1,0:T(8,128)(2,1)S(1)} %bitcast.69), kind=kOutput, calls=%fused_computation.42 | convolution fusion | flops 603979776 | bytes 4718592 | tf_op jit(solution)/shard_map/kij,kjc->kic/dot_general | solution.py:28
  25.6 1.6 copy.10
  27.2 3.4 %fusion.5 = f32[1536,256]{0,1:T(8,128)S(1)} fusion(f32[1536,256]{0,1:T(8,128)} %copy.10, bf16[1536,256]{0,1:T(8,128)(2,1)S(1)} %copy.9, bf16[1,1536,256]{2,1,0:T(8,128)(2,1)} %all-gather.1, bf16[1,1536,256]{2,1,0:T(8,128)(2,1)} %all-gather), kind=kOutput, calls=%fused_computation.10 | convolution fusion | flops 405078016 | bytes 5505024 | tf_op jit(solution)/shard_map/dot_general | solution.py:42
  30.7 0.4 convolution_bitcast_fusion.8
  31.1 1.8 %collective-permute-start = (f32[256,256]{0,1:T(8,128)S(1)}, f32[256,256]{0,1:T(8,128)S(1)}, u32[]{:S(2)}, u32[]{:S(2)}) collective-permute-start(f32[256,256]{0,1:T(8,128)S(1)} %convolution_bitcast_fusion.8), channel_id=1, source_target_pairs={{0,2},{2,0},{4,6},{6,4},{8,10},{10,8},{12,14},{14,12},{16,18},{18,... | collective-permute-start | bytes 786440 | tf_op jit(solution)/shard_map/ppermute | solution.py:12
  32.9 2.4 %all-gather.3 = bf16[1,1536,256]{2,1,0:T(8,128)(2,1)S(1)} all-gather(bf16[1,1536,128]{2,1,0:T(8,128)(2,1)S(1)} %copy-done.8), channel_id=5, replica_groups=mesh['rows'=16,'cols'=2] {'cols'}, dimensions={2}, use_global_device_ids=true | all-gather | bytes 1179648 | tf_op jit(solution)/shard_map/all_gather | solution.py:43
  35.2 2.4 %all-gather.4 = bf16[1,1536,256]{2,1,0:T(8,128)(2,1)S(1)} all-gather(bf16[1,1536,128]{2,1,0:T(8,128)(2,1)S(1)} %copy-done.9), channel_id=6, replica_groups=mesh['rows'=16,'cols'=2] {'cols'}, dimensions={2}, use_global_device_ids=true | all-gather | bytes 1179648 | tf_op jit(solution)/shard_map/all_gather | solution.py:35
  37.6 2.1 %collective-permute-done = f32[256,256]{0,1:T(8,128)S(1)} collective-permute-done((f32[256,256]{0,1:T(8,128)S(1)}, f32[256,256]{0,1:T(8,128)S(1)}, u32[]{:S(2)}, u32[]{:S(2)}) %collective-permute-start) | collective-permute-done | bytes 262176 | tf_op jit(solution)/shard_map/ppermute | solution.py:12
  39.7 0.4 fusion.4
  40.1 0.4 convolution_bitcast_fusion.7
  40.5 1.8 %collective-permute-start.1 = (f32[256,256]{0,1:T(8,128)S(1)}, f32[256,256]{0,1:T(8,128)S(1)}, u32[]{:S(2)}, u32[]{:S(2)}) collective-permute-start(f32[256,256]{0,1:T(8,128)S(1)} %convolution_bitcast_fusion.7), channel_id=1, source_target_pairs={{0,2},{2,0},{4,6},{6,4},{8,10},{10,8},{12,14},{14,12},{16,18},{18,... | collective-permute-start | bytes 786440 | tf_op jit(solution)/shard_map/ppermute | solution.py:12
  42.3 6.0 %collective-permute-done.1 = f32[256,256]{0,1:T(8,128)S(1)} collective-permute-done((f32[256,256]{0,1:T(8,128)S(1)}, f32[256,256]{0,1:T(8,128)S(1)}, u32[]{:S(2)}, u32[]{:S(2)}) %collective-permute-start.1) | collective-permute-done | bytes 262176 | tf_op jit(solution)/shard_map/ppermute | solution.py:12
  48.3 1.8 %collective-permute-start.2 = (f32[256,256]{0,1:T(8,128)S(1)}, f32[256,256]{0,1:T(8,128)S(1)}, u32[]{:S(2)}, u32[]{:S(2)}) collective-permute-start(f32[256,256]{0,1:T(8,128)S(1)} %add.48), channel_id=1, source_target_pairs={{0,4},{2,6},{4,0},{6,2},{8,12},{10,14},{12,8},{14,10},{16,20},{18,... | collective-permute-start | bytes 786440 | tf_op jit(solution)/shard_map/ppermute | solution.py:12
  50.1 2.4 %all-gather.5 = bf16[1,1536,256]{2,1,0:T(8,128)(2,1)S(1)} all-gather(bf16[1,1536,128]{2,1,0:T(8,128)(2,1)S(1)} %copy-done.6), channel_id=7, replica_groups=mesh['rows'=16,'cols'=2] {'cols'}, dimensions={2}, use_global_device_ids=true | all-gather | bytes 1179648 | tf_op jit(solution)/shard_map/all_gather | solution.py:43
  52.4 2.4 %all-gather.6 = bf16[1,1536,256]{2,1,0:T(8,128)(2,1)S(1)} all-gather(bf16[1,1536,128]{2,1,0:T(8,128)(2,1)S(1)} %copy-done.7), channel_id=8, replica_groups=mesh['rows'=16,'cols'=2] {'cols'}, dimensions={2}, use_global_device_ids=true | all-gather | bytes 1179648 | tf_op jit(solution)/shard_map/all_gather | solution.py:35
  55.1 0.4 fusion.3
  55.9 1.8 %collective-permute-start.3 = (f32[256,256]{0,1:T(8,128)S(1)}, f32[256,256]{0,1:T(8,128)S(1)}, u32[]{:S(2)}, u32[]{:S(2)}) collective-permute-start(f32[256,256]{0,1:T(8,128)S(1)} %convolution_bitcast_fusion.6), channel_id=1, source_target_pairs={{0,2},{2,0},{4,6},{6,4},{8,10},{10,8},{12,14},{14,12},{16,18},{18,... | collective-permute-start | bytes 786440 | tf_op jit(solution)/shard_map/ppermute | solution.py:12
  57.7 6.3 %collective-permute-done.3 = f32[256,256]{0,1:T(8,128)S(1)} collective-permute-done((f32[256,256]{0,1:T(8,128)S(1)}, f32[256,256]{0,1:T(8,128)S(1)}, u32[]{:S(2)}, u32[]{:S(2)}) %collective-permute-start.3) | collective-permute-done | bytes 262176 | tf_op jit(solution)/shard_map/ppermute | solution.py:12
  64.4 6.9 %collective-permute-done.4 = f32[256,256]{0,1:T(8,128)S(1)} collective-permute-done((f32[256,256]{0,1:T(8,128)S(1)}, f32[256,256]{0,1:T(8,128)S(1)}, u32[]{:S(2)}, u32[]{:S(2)}) %collective-permute-start.4) | collective-permute-done | bytes 262176 | tf_op jit(solution)/shard_map/ppermute | solution.py:12
  71.3 1.3 collective-permute-start.5
  72.6 2.4 %all-gather.7 = bf16[1,1536,256]{2,1,0:T(8,128)(2,1)S(1)} all-gather(bf16[1,1536,128]{2,1,0:T(8,128)(2,1)S(1)} %copy-done.5), channel_id=9, replica_groups=mesh['rows'=16,'cols'=2] {'cols'}, dimensions={2}, use_global_device_ids=true | all-gather | bytes 1179648 | tf_op jit(solution)/shard_map/all_gather | solution.py:43
  74.9 2.4 %all-gather.8 = bf16[1,1536,256]{2,1,0:T(8,128)(2,1)S(1)} all-gather(bf16[1,1536,128]{2,1,0:T(8,128)(2,1)S(1)} %get-tuple-element.8), channel_id=10, replica_groups=mesh['rows'=16,'cols'=2] {'cols'}, dimensions={2}, use_global_device_ids=true | all-gather | bytes 1179648 | tf_op jit(solution)/shard_map/all_gather | solution.py:35
  77.3 0.5 collective-permute-done.5
  77.7 0.4 fusion.2
  78.1 0.4 convolution_bitcast_fusion.5
  78.5 1.2 collective-permute-start.6
  79.8 6.7 %collective-permute-done.6 = f32[256,256]{0,1:T(8,128)S(1)} collective-permute-done((f32[256,256]{0,1:T(8,128)S(1)}, f32[256,256]{0,1:T(8,128)S(1)}, u32[]{:S(2)}, u32[]{:S(2)}) %collective-permute-start.6) | collective-permute-done | bytes 262176 | tf_op jit(solution)/shard_map/ppermute | solution.py:12
  86.9 6.7 %collective-permute-done.7 = f32[256,256]{0,1:T(8,128)S(1)} collective-permute-done((f32[256,256]{0,1:T(8,128)S(1)}, f32[256,256]{0,1:T(8,128)S(1)}, u32[]{:S(2)}, u32[]{:S(2)}) %collective-permute-start.7) | collective-permute-done | bytes 262176 | tf_op jit(solution)/shard_map/ppermute | solution.py:12
  93.6 0.5 collective-permute-start.8
  94.1 5.9 %collective-permute-done.8 = f32[256,256]{0,1:T(8,128)S(1)} collective-permute-done((f32[256,256]{0,1:T(8,128)S(1)}, f32[256,256]{0,1:T(8,128)S(1)}, u32[]{:S(2)}, u32[]{:S(2)}) %collective-permute-start.8) | collective-permute-done | bytes 262176 | tf_op jit(solution)/shard_map/ppermute | solution.py:12
  100.1 0.7 add.55
  100.8 3.1 %collective-permute-start.9 = (f32[256,256]{0,1:T(8,128)}, f32[256,256]{0,1:T(8,128)}, u32[]{:S(2)}, u32[]{:S(2)}) collective-permute-start(f32[256,256]{0,1:T(8,128)} %add.55), channel_id=1, source_target_pairs={{0,16},{2,18},{4,20},{6,22},{8,24},{10,26},{12,28},{14,30},{16,0},... | collective-permute-start | bytes 786440 | tf_op jit(solution)/shard_map/ppermute | solution.py:12
  103.9 1.4 copy.8
  105.3 2.4 %all-gather.9 = bf16[1,1536,256]{2,1,0:T(8,128)(2,1)S(1)} all-gather(bf16[1,1536,128]{2,1,0:T(8,128)(2,1)S(1)} %copy-done.4), channel_id=11, replica_groups=mesh['rows'=16,'cols'=2] {'cols'}, dimensions={2}, use_global_device_ids=true | all-gather | bytes 1179648 | tf_op jit(solution)/shard_map/all_gather | solution.py:43
  107.7 5.3 %collective-permute-done.9 = f32[256,256]{0,1:T(8,128)} collective-permute-done((f32[256,256]{0,1:T(8,128)}, f32[256,256]{0,1:T(8,128)}, u32[]{:S(2)}, u32[]{:S(2)}) %collective-permute-start.9) | collective-permute-done | bytes 262176 | tf_op jit(solution)/shard_map/ppermute | solution.py:12
  113.0 2.8 %multiply_reduce_fusion = (f32[256]{0:T(256)S(1)}, f32[256]{0:T(256)S(1)}, f32[1536,256]{0,1:T(8,128)}) fusion(bf16[1536,256]{0,1:T(8,128)(2,1)S(1)} %copy.9, f32[1536,256]{0,1:T(8,128)S(1)} %fusion.2, bf16[1,1536,256]{2,1,0:T(8,128)(2,1)S(1)} %all-gather.9, f32[256,256]{0,1:T(8,128)} %add.55, f32[256,256]{0,1:T(8,128)} %collective-permute-done.9, ...), kind=kOutput, calls=%fused_computation.14 | convolution fusion | flops 204602880 | bytes 6031360 | tf_op jit(solution)/shard_map/dot_general | solution.py:42
  115.8 3.0 %copy.11 = f32[1536,256]{1,0:T(8,128)} copy(f32[1536,256]{0,1:T(8,128)} %get-tuple-element.18) | data formatting | bytes 3145728
  118.8 40.2 %all-reduce = (f32[256]{0:T(256)S(1)}, f32[256]{0:T(256)S(1)}) all-reduce(f32[256]{0:T(256)S(1)} %get-tuple-element.5, f32[256]{0:T(256)S(1)} %get-tuple-element.4), channel_id=1, replica_groups=mesh['rows'=16,'cols'=2] {'rows'}, use_global_device_ids=true, to_apply=%region_1.0 | all-reduce | flops 512 | bytes 4096 | tf_op jit(solution)/shard_map/psum | solution.py:51
  159.0 0.6 divide_add_fusion
  (31 shorter events, 1.9 us)
Async XLA Ops:
  7.2 1.1 copy-start
  7.2 1.8 %copy-start.2 = (bf16[5,1536,128]{2,1,0:T(8,128)(2,1)S(1)}, bf16[5,1536,128]{2,1,0:T(8,128)(2,1)}, u32[]{:S(2)}) copy-start(bf16[5,1536,128]{2,1,0:T(8,128)(2,1)} %param.10) | copy-start | bytes 5898244
  7.2 16.0 %all-gather.12.cloned.1.call-start = ((), (), s32[]{:S(2)}) async-start(), calls=%async_computation | async-start | bytes 3538944 | tf_op jit(solution)/shard_map/all_gather | solution.py:26
  9.0 3.8 %copy-start.3 = (bf16[5,1536,128]{2,1,0:T(8,128)(2,1)S(1)}, bf16[5,1536,128]{2,1,0:T(8,128)(2,1)}, u32[]{:S(2)}) copy-start(bf16[5,1536,128]{2,1,0:T(8,128)(2,1)} %param.9) | copy-start | bytes 5898244
  27.2 3.4 %copy-start.1 = (bf16[1,1536,256]{2,1,0:T(8,128)(2,1)S(1)}, bf16[1,1536,256]{2,1,0:T(8,128)(2,1)}, u32[]{:S(2)}) copy-start(bf16[1,1536,256]{2,1,0:T(8,128)(2,1)} %all-gather.2) | copy-start | bytes 2359300
  30.7 2.2 %copy-start.8 = (bf16[1,1536,128]{2,1,0:T(8,128)(2,1)S(1)}, bf16[1,1536,128]{2,1,0:T(8,128)(2,1)}, u32[]{:S(2)}) copy-start(bf16[1,1536,128]{2,1,0:T(8,128)(2,1)} %get-tuple-element.15) | copy-start | bytes 1179652
  30.7 4.5 %copy-start.9 = (bf16[1,1536,128]{2,1,0:T(8,128)(2,1)S(1)}, bf16[1,1536,128]{2,1,0:T(8,128)(2,1)}, u32[]{:S(2)}) copy-start(bf16[1,1536,128]{2,1,0:T(8,128)(2,1)} %get-tuple-element.9) | copy-start | bytes 1179652
  31.1 8.6 %collective-permute-start = (f32[256,256]{0,1:T(8,128)S(1)}, f32[256,256]{0,1:T(8,128)S(1)}, u32[]{:S(2)}, u32[]{:S(2)}) collective-permute-start(f32[256,256]{0,1:T(8,128)S(1)} %convolution_bitcast_fusion.8), channel_id=1, source_target_pairs={{0,2},{2,0},{4,6},{6,4},{8,10},{10,8},{12,14},{14,12},{16,18},{18,... | collective-permute-start | bytes 786440 | tf_op jit(solution)/shard_map/ppermute | solution.py:12
  40.1 10.0 %copy-start.6 = (bf16[1,1536,128]{2,1,0:T(8,128)(2,1)S(1)}, bf16[1,1536,128]{2,1,0:T(8,128)(2,1)}, u32[]{:S(2)}) copy-start(bf16[1,1536,128]{2,1,0:T(8,128)(2,1)} %get-tuple-element.14) | copy-start | bytes 1179652
  40.5 12.0 %copy-start.7 = (bf16[1,1536,128]{2,1,0:T(8,128)(2,1)S(1)}, bf16[1,1536,128]{2,1,0:T(8,128)(2,1)}, u32[]{:S(2)}) copy-start(bf16[1,1536,128]{2,1,0:T(8,128)(2,1)} %get-tuple-element.12) | copy-start | bytes 1179652
  40.5 7.8 %collective-permute-start.1 = (f32[256,256]{0,1:T(8,128)S(1)}, f32[256,256]{0,1:T(8,128)S(1)}, u32[]{:S(2)}, u32[]{:S(2)}) collective-permute-start(f32[256,256]{0,1:T(8,128)S(1)} %convolution_bitcast_fusion.7), channel_id=1, source_target_pairs={{0,2},{2,0},{4,6},{6,4},{8,10},{10,8},{12,14},{14,12},{16,18},{18,... | collective-permute-start | bytes 786440 | tf_op jit(solution)/shard_map/ppermute | solution.py:12
  48.3 6.8 %collective-permute-start.2 = (f32[256,256]{0,1:T(8,128)S(1)}, f32[256,256]{0,1:T(8,128)S(1)}, u32[]{:S(2)}, u32[]{:S(2)}) collective-permute-start(f32[256,256]{0,1:T(8,128)S(1)} %add.48), channel_id=1, source_target_pairs={{0,4},{2,6},{4,0},{6,2},{8,12},{10,14},{12,8},{14,10},{16,20},{18,... | collective-permute-start | bytes 786440 | tf_op jit(solution)/shard_map/ppermute | solution.py:12
  55.5 17.0 %copy-start.5 = (bf16[1,1536,128]{2,1,0:T(8,128)(2,1)S(1)}, bf16[1,1536,128]{2,1,0:T(8,128)(2,1)}, u32[]{:S(2)}) copy-start(bf16[1,1536,128]{2,1,0:T(8,128)(2,1)} %get-tuple-element.17) | copy-start | bytes 1179652
  55.9 8.1 %collective-permute-start.3 = (f32[256,256]{0,1:T(8,128)S(1)}, f32[256,256]{0,1:T(8,128)S(1)}, u32[]{:S(2)}, u32[]{:S(2)}) collective-permute-start(f32[256,256]{0,1:T(8,128)S(1)} %convolution_bitcast_fusion.6), channel_id=1, source_target_pairs={{0,2},{2,0},{4,6},{6,4},{8,10},{10,8},{12,14},{14,12},{16,18},{18,... | collective-permute-start | bytes 786440 | tf_op jit(solution)/shard_map/ppermute | solution.py:12
  64.0 7.2 %collective-permute-start.4 = (f32[256,256]{0,1:T(8,128)S(1)}, f32[256,256]{0,1:T(8,128)S(1)}, u32[]{:S(2)}, u32[]{:S(2)}) collective-permute-start(f32[256,256]{0,1:T(8,128)S(1)} %add.50), channel_id=1, source_target_pairs={{0,4},{2,6},{4,0},{6,2},{8,12},{10,14},{12,8},{14,10},{16,20},{18,... | collective-permute-start | bytes 786440 | tf_op jit(solution)/shard_map/ppermute | solution.py:12
  71.3 6.4 %collective-permute-start.5 = (f32[256,256]{0,1:T(8,128)S(1)}, f32[256,256]{0,1:T(8,128)S(1)}, u32[]{:S(2)}, u32[]{:S(2)}) collective-permute-start(f32[256,256]{0,1:T(8,128)S(1)} %add.51), channel_id=1, source_target_pairs={{0,8},{2,10},{4,12},{6,14},{8,0},{10,2},{12,4},{14,6},{16,24},{18,... | collective-permute-start | bytes 786440 | tf_op jit(solution)/shard_map/ppermute | solution.py:12
  78.5 8.0 %collective-permute-start.6 = (f32[256,256]{0,1:T(8,128)S(1)}, f32[256,256]{0,1:T(8,128)S(1)}, u32[]{:S(2)}, u32[]{:S(2)}) collective-permute-start(f32[256,256]{0,1:T(8,128)S(1)} %convolution_bitcast_fusion.5), channel_id=1, source_target_pairs={{0,2},{2,0},{4,6},{6,4},{8,10},{10,8},{12,14},{14,12},{16,18},{18,... | collective-permute-start | bytes 786440 | tf_op jit(solution)/shard_map/ppermute | solution.py:12
  86.5 18.8 %copy-start.4 = (bf16[1,1536,128]{2,1,0:T(8,128)(2,1)S(1)}, bf16[1,1536,128]{2,1,0:T(8,128)(2,1)}, u32[]{:S(2)}) copy-start(bf16[1,1536,128]{2,1,0:T(8,128)(2,1)} %get-tuple-element.13) | copy-start | bytes 1179652
  86.5 7.1 %collective-permute-start.7 = (f32[256,256]{0,1:T(8,128)S(1)}, f32[256,256]{0,1:T(8,128)S(1)}, u32[]{:S(2)}, u32[]{:S(2)}) collective-permute-start(f32[256,256]{0,1:T(8,128)S(1)} %add.53), channel_id=1, source_target_pairs={{0,4},{2,6},{4,0},{6,2},{8,12},{10,14},{12,8},{14,10},{16,20},{18,... | collective-permute-start | bytes 786440 | tf_op jit(solution)/shard_map/ppermute | solution.py:12
  93.6 6.4 %collective-permute-start.8 = (f32[256,256]{0,1:T(8,128)S(1)}, f32[256,256]{0,1:T(8,128)S(1)}, u32[]{:S(2)}, u32[]{:S(2)}) collective-permute-start(f32[256,256]{0,1:T(8,128)S(1)} %add.54), channel_id=1, source_target_pairs={{0,8},{2,10},{4,12},{6,14},{8,0},{10,2},{12,4},{14,6},{16,24},{18,... | collective-permute-start | bytes 786440 | tf_op jit(solution)/shard_map/ppermute | solution.py:12
  100.8 12.2 %collective-permute-start.9 = (f32[256,256]{0,1:T(8,128)}, f32[256,256]{0,1:T(8,128)}, u32[]{:S(2)}, u32[]{:S(2)}) collective-permute-start(f32[256,256]{0,1:T(8,128)} %add.55), channel_id=1, source_target_pairs={{0,16},{2,18},{4,20},{6,22},{8,24},{10,26},{12,28},{14,30},{16,0},... | collective-permute-start | bytes 786440 | tf_op jit(solution)/shard_map/ppermute | solution.py:12
  115.8 43.2 %copy-start.10 = (f32[256]{0:T(256)S(1)}, f32[256]{0:T(256)}, u32[]{:S(2)}) copy-start(f32[256]{0:T(256)} %param.11) | copy-start | bytes 3076
Sparse Core Ops, SparseCore 0:
  9.6 13.5 all-gather.11
where the time goes:
time: 167 us; the launch traced here: 166 us
  blocking collectives  64.3 us (39%)
  waiting for transfers between devices  51.7 us (31%)
  between operations  14.2 us (9%)
  starting transfers between devices  14 us (8%)
  matrix products  11.4 us (7%)
  local copies, waits for them, and re-layouts  9.41 us (6%)
    ppermute x10, waiting for transfers between devices, partner(): return lax.ppermute(value, axis, pairs)  46.6 us
    psum x1, blocking collectives, per_device(): lax.psum((numerator_local, denominator_local), 'rows')  40.2 us
    ppermute x10, starting transfers between devices, partner(): return lax.ppermute(value, axis, pairs)  14 us
    all_gather x5, blocking collectives, per_device(): lax.all_gather(bases_v[level_index], 'cols', axis=1, tiled=True)  12.1 us
    all_gather x5, blocking collectives, per_device(): lax.all_gather(bases_u[level_index], 'cols', axis=1, tiled=True)  12 us
    dot_general x5, matrix products, per_device(): jnp.dot(lax.all_gather(bases_u[level_index], 'cols', axis=1, tiled=True),...  7.46 us
    unnamed x25, local copies, waits for them, and re-layouts  5.52 us
    all_gather x1, waiting for transfers between devices, per_device(): leaf_segment = lax.all_gather(leaf_offset, 'cols', axis=1, tiled=True)  4.4 us
  transfers between devices with their start and end apart: 11, of which 11 were waited for; matrix products, arithmetic and copies ran while one was open for 2% of the time, Pallas kernels for 0%

commit v1 on v0

v1 whole, which is shorter than its diff:
```python
import functools

import jax
import jax.numpy as jnp
from jax import lax
from jax.experimental import pallas as pl
from jax.experimental.pallas import tpu as pltpu
from jax.sharding import PartitionSpec as P

epsilon = 1e-06
MESH = pl.DeviceIdType.MESH
MOST = 16


def log2(value):
    return value.bit_length() - 1


def tdot(a, b):
    return lax.dot_general(a, b, (((0,), (0,)), ((), ())), preferred_element_type=jnp.float32)


def dot(a, b):
    return jnp.dot(a, b, preferred_element_type=jnp.float32)


def kernel(n, it_h, r_h, leaf_h, v_h, u_h, est_ref, out_h, fun_ref,
           it, r, rp, leaf, v, u, x, pf, ps, rs, c, xs, xr, st, sg, sx,
           lsem, wsend, wrecv, ssem, rsem, xsem, osem):
    rows, vecs = r.shape
    rank = v.shape[2]
    half = rank // 2
    width = leaf.shape[1]
    lh = width // 2
    top = log2(n)
    most = min(n, MOST)
    me = lax.axis_index("rows")
    col = lax.axis_index("cols")
    other = 1 - col

    local = []

    def fetch(src, dst, slot):
        copy = pltpu.make_async_copy(src, dst, lsem.at[slot])
        copy.start()
        return copy

    base = 0
    got_r = []
    for k in range(rows // width):
        for part, which in enumerate((col, other)):
            start = pl.multiple_of(k * width + which * lh, 16)
            got_r.append(fetch(r_h.at[pl.ds(start, lh)], rp.at[pl.ds(k * width + part * lh, lh)], base))
            base += 1
    got_r.append(fetch(r_h, r, base))
    got_leaf = fetch(leaf_h, leaf.at[:, pl.ds(0, lh)], base + 1)
    base += 2
    got_v, got_u = {}, {}
    for l in range(top, -1, -1):
        got_v[l] = fetch(v_h.at[l], v.at[l, :, pl.ds(0, half)], base)
        got_u[l] = fetch(u_h.at[l], u.at[l, :, pl.ds(0, half)], base + 1)
        base += 2
    got_it = fetch(it_h, it, base)

    barrier = pltpu.get_barrier_semaphore()
    pl.semaphore_signal(barrier, inc=1, device_id={"cols": other}, device_id_type=MESH)
    peers = list(range(1, most)) + [most << b for b in range(log2(n // most))]
    for o in peers:
        pl.semaphore_signal(barrier, inc=1, device_id={"rows": me ^ o}, device_id_type=MESH)
    pl.semaphore_wait(barrier, len(peers) + 1)

    sends = []

    def push(src, dst, slot):
        copy = pltpu.make_async_remote_copy(
            src_ref=src, dst_ref=dst, send_sem=wsend.at[slot], recv_sem=wrecv.at[slot],
            device_id={"cols": other}, device_id_type=MESH)
        copy.start()
        sends.append(copy)
        return copy

    in_leaf = push(leaf_h, leaf.at[:, pl.ds(lh, lh)], 0)
    in_v, in_u = {}, {}
    for l in range(top, -1, -1):
        in_v[l] = push(v_h.at[l], v.at[l, :, pl.ds(half, half)], 1 + 2 * l)
        in_u[l] = push(u_h.at[l], u.at[l, :, pl.ds(half, half)], 2 + 2 * l)

    def ready_v(l):
        got_v[l].wait()
        in_v[l].wait_recv()

    def ready_u(l):
        got_u[l].wait()
        in_u[l].wait_recv()

    def send(src, dst, l, phase, o):
        copy = pltpu.make_async_remote_copy(
            src_ref=src, dst_ref=dst, send_sem=ssem.at[l, phase, o], recv_sem=rsem.at[l, phase, o],
            device_id={"rows": me ^ o}, device_id_type=MESH)
        copy.start()
        sends.append(copy)
        return copy

    def send_far(src, dst, l, b):
        copy = pltpu.make_async_remote_copy(
            src_ref=src, dst_ref=dst, send_sem=xsem.at[0, l, b], recv_sem=xsem.at[1, l, b],
            device_id={"rows": me ^ (most << b)}, device_id_type=MESH)
        copy.start()
        sends.append(copy)
        copy.wait_recv()

    for copy in got_r:
        copy.wait()
    got_leaf.wait()
    in_leaf.wait_recv()
    for k in range(rows // width):
        s = pl.ds(k * width, width)
        x[s] = r[s].astype(jnp.float32) + dot(leaf[s], rp[s])
    ready_v(top)
    narrow = tdot(v[top], x[...].astype(jnp.bfloat16)).astype(jnp.bfloat16)
    ready_u(top)
    x[...] = x[...] - dot(u[top], narrow)
    ready_v(top - 1)
    partial = tdot(v[top - 1], x[...].astype(jnp.bfloat16))

    for l in range(top - 1, -1, -1):
        group = 2 ** (top - l)
        h = min(group, most)
        pair = h == 2
        ch = rank if pair else rank // h
        j = me & (h - 1)
        mine = pl.ds(pl.multiple_of(j * ch, 16), ch)
        ps[l] = partial.astype(jnp.bfloat16)
        if pair:
            moved = [send(ps.at[l], rs.at[l], l, 0, 1)]
        else:
            moved = [
                send(ps.at[l, pl.ds(pl.multiple_of((j ^ o) * ch, 16), ch)],
                     rs.at[l, pl.ds((o - 1) * ch, ch)], l, 0, o)
                for o in range(h - 1, 0, -1)
            ]
            pf[...] = partial
        if l < top - 1:
            moved_x = x[...] - dot(u[l + 1], c[l + 1])
            x[...] = it[...].astype(jnp.float32) - moved_x if l == 0 else moved_x
        ready_u(l)
        if l == 1:
            got_it.wait()

        def ahead():
            ready_v(l - 1)
            term = tdot(v[l - 1], x[...].astype(jnp.bfloat16))
            cross = tdot(v[l - 1], u[l]).astype(jnp.bfloat16)
            return term, cross

        if pair:
            term, cross = ahead() if l > 0 else (None, None)
            for copy in moved:
                copy.wait_recv()
            c[l] = (partial + rs[l].astype(jnp.float32)).astype(jnp.bfloat16)
        else:
            for copy in moved:
                copy.wait_recv()
            total = pf[mine]
            for o in range(1, h):
                total = total + rs[l, pl.ds((o - 1) * ch, ch)].astype(jnp.float32)
            for b in range(log2(group // h)):
                xs[l, b] = total
                send_far(xs.at[l, b], xr.at[l, b], l, b)
                total = total + xr[l, b]
            c[l, mine] = total.astype(jnp.bfloat16)
            moved = [send(c.at[l, mine], c.at[l, mine], l, 1, o) for o in range(h - 1, 0, -1)]
            term, cross = ahead() if l > 0 else (None, None)
            for copy in moved:
                copy.wait_recv()
        if l > 0:
            partial = term - dot(cross, c[l])

    blocks = 4
    size = rows // blocks
    num = jnp.zeros((1, vecs), jnp.float32)
    den = jnp.zeros((1, vecs), jnp.float32)
    outs = []
    for k in range(blocks):
        s = pl.ds(k * size, size)
        updated = x[s] + dot(u[0, s], c[0])
        x[s] = updated
        copy = pltpu.make_async_copy(x.at[s], out_h.at[s], osem.at[k])
        copy.start()
        outs.append(copy)
        num = num + jnp.sum(updated * r[s].astype(jnp.float32), axis=0, keepdims=True)
        den = den + jnp.sum(updated * updated, axis=0, keepdims=True)
    st[pl.ds(0, 1)] = num
    st[pl.ds(1, 1)] = den
    moved = [send(st, sg.at[o - 1], top, 0, o) for o in range(most - 1, 0, -1)]
    for copy in moved:
        copy.wait_recv()
    total = st[...]
    for o in range(1, most):
        total = total + sg[o - 1]
    for b in range(log2(n // most)):
        sx[b] = total
        send_far(sx.at[b], sx.at[log2(n // most) + b], top, b)
        total = total + sx[log2(n // most) + b]
    fun_ref[...] = est_ref[...] + total[0:1] / (total[1:2] + epsilon)
    for copy in sends:
        copy.wait_send()
    for copy in outs:
        copy.wait()


def per_device(n, iterate, residual, leaf_offset, bases_v, bases_u, estimate):
    rows, vecs = residual.shape
    levels = bases_v.shape[0]
    rank = 2 * bases_v.shape[2]
    width = 2 * leaf_offset.shape[1]
    top = levels - 1
    most = min(n, MOST)
    far = max(log2(n // most), 1)
    hbm = pl.BlockSpec(memory_space=pl.ANY)
    vmem = pl.BlockSpec(memory_space=pltpu.VMEM)
    bf, f32 = jnp.bfloat16, jnp.float32
    updated, functional = pl.pallas_call(
        functools.partial(kernel, n),
        out_shape=(
            jax.ShapeDtypeStruct((rows, vecs), f32),
            jax.ShapeDtypeStruct((1, vecs), f32),
        ),
        in_specs=[hbm] * 5 + [vmem],
        out_specs=(hbm, vmem),
        scratch_shapes=[
            pltpu.VMEM((rows, vecs), bf),
            pltpu.VMEM((rows, vecs), bf),
            pltpu.VMEM((rows, vecs), bf),
            pltpu.VMEM((rows, width), bf),
            pltpu.VMEM((levels, rows, rank), bf),
            pltpu.VMEM((levels, rows, rank), bf),
            pltpu.VMEM((rows, vecs), f32),
            pltpu.VMEM((rank, vecs), f32),
            pltpu.VMEM((top, rank, vecs), bf),
            pltpu.VMEM((top, rank, vecs), bf),
            pltpu.VMEM((top, rank, vecs), bf),
            pltpu.VMEM((top, far, rank // most, vecs), f32),
            pltpu.VMEM((top, far, rank // most, vecs), f32),
            pltpu.VMEM((8, vecs), f32),
            pltpu.VMEM((most, 8, vecs), f32),
            pltpu.VMEM((2 * far, 8, vecs), f32),
            pltpu.SemaphoreType.DMA((2 * (rows // width) + 2 * levels + 3,)),
            pltpu.SemaphoreType.DMA((2 * levels + 1,)),
            pltpu.SemaphoreType.DMA((2 * levels + 1,)),
            pltpu.SemaphoreType.DMA((levels, 2, most)),
            pltpu.SemaphoreType.DMA((levels, 2, most)),
            pltpu.SemaphoreType.DMA((2, levels, far)),
            pltpu.SemaphoreType.DMA((4,)),
        ],
        compiler_params=pltpu.CompilerParams(
            collective_id=0, has_side_effects=True, vmem_limit_bytes=56 << 20
        ),
    )(iterate, residual, leaf_offset, bases_v, bases_u, estimate.reshape(1, vecs))
    return updated, functional.reshape(vecs)


def solution(mesh):
    return jax.shard_map(
        functools.partial(per_device, mesh.shape["rows"]),
        mesh=mesh,
        in_specs=(
            P("rows", "cols"),
            P("rows", "cols"),
            P("rows", "cols"),
            P(None, "rows", "cols"),
            P(None, "rows", "cols"),
            P("cols"),
        ),
        out_specs=(P("rows", "cols"), P("cols")),
        check_vma=False,
    )
```

time: 167 us -> 57.2 us (0.34)
  blocking collectives: 64.3 us -> 0 us
  Pallas kernels: 0 us -> 53.1 us
  waiting for transfers between devices: 51.7 us -> 0 us
  starting transfers between devices: 14 us -> 0 us
  between operations: 14.2 us -> 0.65 us
  matrix products: 11.4 us -> 0 us
  local copies, waits for them, and re-layouts: 9.41 us -> 3.22 us
    pallas_call x0 -> x1, Pallas kernels: none -> 53.1 us  [per_device(): pl.pallas_call(functools.partial(kernel, n), out_shape=(jax.ShapeDtypeStr...]
    ppermute x10 -> x0, waiting for transfers between devices: 46.6 us -> none  [partner(): return lax.ppermute(value, axis, pairs)]
    psum x1 -> x0, blocking collectives: 40.2 us -> none  [per_device(): lax.psum((numerator_local, denominator_local), 'rows')]
    all_gather x10 -> x0, blocking collectives: 24.1 us -> none  [the longest x5 12.1 us: per_device(): lax.all_gather(bases_v[level_index], 'cols', axis=1, tiled=True)]
    ppermute x10 -> x0, starting transfers between devices: 14 us -> none  [partner(): return lax.ppermute(value, axis, pairs)]
    dot_general x10 -> x0, matrix products: 11.4 us -> none  [the longest x5 7.46 us: per_device(): jnp.dot(lax.all_gather(bases_u[level_index], 'cols', axis=1, tiled=True),...]
    all_gather x1 -> x0, waiting for transfers between devices: 4.4 us -> none  [per_device(): leaf_segment = lax.all_gather(leaf_offset, 'cols', axis=1, tiled=True)]
    unnamed x25 -> x4, local copies, waits for them, and re-layouts: 5.52 us -> 3.22 us
  transfers between devices with their start and end apart: 11 -> 0, of which waited for: 11 -> 0; matrix products, arithmetic and copies ran while one was open for 2% -> 0% of each run, Pallas kernels for 0% -> 0%
where the time goes in v1:
time: 57.2 us; the launch traced here: 57 us
  Pallas kernels  53.1 us (93%)
  local copies, waits for them, and re-layouts  3.22 us (6%)
  between operations  0.65 us (1%)
    pallas_call x1, Pallas kernels, per_device(): pl.pallas_call(functools.partial(kernel, n), out_shape=(jax.ShapeDtypeStr...  53.1 us
    unnamed x4, local copies, waits for them, and re-layouts  3.22 us

profile of v1, /device:TPU:0, one launch (start us, length us, event | category | flops | bytes accessed | tf_op | source)
XLA Modules:
  0.0 57.0 jit_solution(6801865257632330852)
XLA Ops:
  0.6 53.1 %shard_map.77 = (f32[1536,256]{1,0:T(8,128)}, f32[1,256]{1,0:T(1,128)}) custom-call(bf16[1536,256]{1,0:T(8,128)(2,1)} %it_h.1, bf16[1536,256]{1,0:T(8,128)(2,1)} %r_h.1, bf16[1536,384]{1,0:T(8,128)(2,1)} %leaf_h.1, bf16[5,1536,128]{2,1,0:T(8,128)(2,1)} %v_h.1, bf16[5,1536,128]{2,1,0:T(8,128)(2,1)} %u_h.1, f32[1,256]{1,0:T(1,128)} %bitcast.3), custom_call_target="tpu_custom_call" | custom-call | tf_op jit(solution)/shard_map/pallas_call | solution.py:223
  53.8 0.0 copy-start
  53.8 2.7 %copy.10 = f32[1536,256]{1,0:T(8,128)} copy(f32[1536,256]{1,0:T(8,128)} %get-tuple-element.8) | data formatting | bytes 3145728
  56.4 0.0 copy-done
  56.4 0.6 copy.11
Async XLA Ops:
  53.8 2.7 %copy-start = (f32[1,256]{1,0:T(1,128)S(1)}, f32[1,256]{1,0:T(1,128)}, u32[]{:S(2)}) copy-start(f32[1,256]{1,0:T(1,128)} %get-tuple-element.5) | copy-start | bytes 3076

commit v2 on v1

--- a/solution.py
+++ b/solution.py
@@ -9,7 +9,7 @@
 
 epsilon = 1e-06
 MESH = pl.DeviceIdType.MESH
-MOST = 16
+MOST = 8
 
 
 def log2(value):
@@ -81,9 +81,18 @@
 
     in_leaf = push(leaf_h, leaf.at[:, pl.ds(lh, lh)], 0)
     in_v, in_u = {}, {}
-    for l in range(top, -1, -1):
+
+    def push_v(l):
         in_v[l] = push(v_h.at[l], v.at[l, :, pl.ds(half, half)], 1 + 2 * l)
+
+    def push_u(l):
         in_u[l] = push(u_h.at[l], u.at[l, :, pl.ds(half, half)], 2 + 2 * l)
+
+    push_v(top)
+    push_u(top)
+    push_v(top - 1)
+    push_u(top - 1)
+    push_v(top - 2)
 
     def ready_v(l):
         got_v[l].wait()
@@ -140,6 +149,10 @@
                 for o in range(h - 1, 0, -1)
             ]
             pf[...] = partial
+        if l > 0:
+            push_u(l - 1)
+        if l > 1:
+            push_v(l - 2)
         if l < top - 1:
             moved_x = x[...] - dot(u[l + 1], c[l + 1])
             x[...] = it[...].astype(jnp.float32) - moved_x if l == 0 else moved_x
@@ -242,9 +255,9 @@
             pltpu.VMEM((top, rank, vecs), bf),
             pltpu.VMEM((top, far, rank // most, vecs), f32),
             pltpu.VMEM((top, far, rank // most, vecs), f32),
-            pltpu.VMEM((8, vecs), f32),
-            pltpu.VMEM((most, 8, vecs), f32),
-            pltpu.VMEM((2 * far, 8, vecs), f32),
+            pltpu.VMEM((2, vecs), f32),
+            pltpu.VMEM((most, 2, vecs), f32),
+            pltpu.VMEM((2 * far, 2, vecs), f32),
             pltpu.SemaphoreType.DMA((2 * (rows // width) + 2 * levels + 3,)),
             pltpu.SemaphoreType.DMA((2 * levels + 1,)),
             pltpu.SemaphoreType.DMA((2 * levels + 1,)),

time: 57.2 us -> 55.4 us (0.969)
  Pallas kernels: 53.1 us -> 51.4 us
    pallas_call x1, Pallas kernels: 53.1 us -> 51.4 us  [per_device(): pl.pallas_call(functools.partial(kernel, n), out_shape=(jax.ShapeDtypeStr...]
where the time goes in v2:
time: 55.4 us; the launch traced here: 55.3 us
  Pallas kernels  51.4 us (93%)
  local copies, waits for them, and re-layouts  3.22 us (6%)
  between operations  0.65 us (1%)
    pallas_call x1, Pallas kernels, per_device(): pl.pallas_call(functools.partial(kernel, n), out_shape=(jax.ShapeDtypeStr...  51.4 us
    unnamed x4, local copies, waits for them, and re-layouts  3.22 us

profile of v2, /device:TPU:0, one launch (start us, length us, event | category | flops | bytes accessed | tf_op | source)
XLA Modules:
  0.0 55.3 jit_solution(9877429426820244543)
XLA Ops:
  0.6 51.4 %shard_map.77 = (f32[1536,256]{1,0:T(8,128)}, f32[1,256]{1,0:T(1,128)}) custom-call(bf16[1536,256]{1,0:T(8,128)(2,1)} %it_h.1, bf16[1536,256]{1,0:T(8,128)(2,1)} %r_h.1, bf16[1536,384]{1,0:T(8,128)(2,1)} %leaf_h.1, bf16[5,1536,128]{2,1,0:T(8,128)(2,1)} %v_h.1, bf16[5,1536,128]{2,1,0:T(8,128)(2,1)} %u_h.1, f32[1,256]{1,0:T(1,128)} %bitcast.3), custom_call_target="tpu_custom_call" | custom-call | tf_op jit(solution)/shard_map/pallas_call | solution.py:236
  52.0 0.0 copy-start
  52.0 2.7 %copy.10 = f32[1536,256]{1,0:T(8,128)} copy(f32[1536,256]{1,0:T(8,128)} %get-tuple-element.8) | data formatting | bytes 3145728
  54.7 0.0 copy-done
  54.7 0.6 %copy.11 = f32[256]{0:T(256)} copy(f32[256]{0:T(256)S(1)} %bitcast.2) | data formatting | bytes 2048
Async XLA Ops:
  52.0 2.7 %copy-start = (f32[1,256]{1,0:T(1,128)S(1)}, f32[1,256]{1,0:T(1,128)}, u32[]{:S(2)}) copy-start(f32[1,256]{1,0:T(1,128)} %get-tuple-element.5) | copy-start | bytes 3076

commit v3 on v2

--- a/solution.py
+++ b/solution.py
@@ -55,44 +55,45 @@
     got_r.append(fetch(r_h, r, base))
     got_leaf = fetch(leaf_h, leaf.at[:, pl.ds(0, lh)], base + 1)
     base += 2
+
+    barrier = pltpu.get_barrier_semaphore()
+    pl.semaphore_signal(barrier, inc=1, device_id={"cols": other}, device_id_type=MESH)
+    peers = list(range(1, most)) + [most << b for b in range(log2(n // most))]
+    for o in peers:
+        pl.semaphore_signal(barrier, inc=1, device_id={"rows": me ^ o}, device_id_type=MESH)
+    pl.semaphore_wait(barrier, len(peers) + 1)
+
+    sends = []
+
+    def push(src, dst, slot):
+        copy = pltpu.make_async_remote_copy(
+            src_ref=src, dst_ref=dst, send_sem=wsend.at[slot], recv_sem=wrecv.at[slot],
+            device_id={"cols": other}, device_id_type=MESH)
+        copy.start()
+        sends.append(copy)
+        return copy
+
+    in_leaf = push(leaf_h, leaf.at[:, pl.ds(lh, lh)], 0)
+    in_v, in_u = {}, {}
+
+    def push_v(l):
+        in_v[l] = push(v_h.at[l], v.at[l, :, pl.ds(half, half)], 1 + 2 * l)
+
+    def push_u(l):
+        in_u[l] = push(u_h.at[l], u.at[l, :, pl.ds(half, half)], 2 + 2 * l)
+
+    push_v(top)
+    push_u(top)
+    push_v(top - 1)
+    push_u(top - 1)
+    push_v(top - 2)
+
     got_v, got_u = {}, {}
     for l in range(top, -1, -1):
         got_v[l] = fetch(v_h.at[l], v.at[l, :, pl.ds(0, half)], base)
         got_u[l] = fetch(u_h.at[l], u.at[l, :, pl.ds(0, half)], base + 1)
         base += 2
     got_it = fetch(it_h, it, base)
-
-    barrier = pltpu.get_barrier_semaphore()
-    pl.semaphore_signal(barrier, inc=1, device_id={"cols": other}, device_id_type=MESH)
-    peers = list(range(1, most)) + [most << b for b in range(log2(n // most))]
-    for o in peers:
-        pl.semaphore_signal(barrier, inc=1, device_id={"rows": me ^ o}, device_id_type=MESH)
-    pl.semaphore_wait(barrier, len(peers) + 1)
-
-    sends = []
-
-    def push(src, dst, slot):
-        copy = pltpu.make_async_remote_copy(
-            src_ref=src, dst_ref=dst, send_sem=wsend.at[slot], recv_sem=wrecv.at[slot],
-            device_id={"cols": other}, device_id_type=MESH)
-        copy.start()
-        sends.append(copy)
-        return copy
-
-    in_leaf = push(leaf_h, leaf.at[:, pl.ds(lh, lh)], 0)
-    in_v, in_u = {}, {}
-
-    def push_v(l):
-        in_v[l] = push(v_h.at[l], v.at[l, :, pl.ds(half, half)], 1 + 2 * l)
-
-    def push_u(l):
-        in_u[l] = push(u_h.at[l], u.at[l, :, pl.ds(half, half)], 2 + 2 * l)
-
-    push_v(top)
-    push_u(top)
-    push_v(top - 1)
-    push_u(top - 1)
-    push_v(top - 2)
 
     def ready_v(l):
         got_v[l].wait()

time: 55.4 us -> 55.4 us (level)
  no operation moved by 1% of the time
where the time goes in v3:
time: 55.4 us; the launch traced here: 55.2 us
  Pallas kernels  51.4 us (93%)
  local copies, waits for them, and re-layouts  3.22 us (6%)
  between operations  0.65 us (1%)
    pallas_call x1, Pallas kernels, per_device(): pl.pallas_call(functools.partial(kernel, n), out_shape=(jax.ShapeDtypeStr...  51.4 us
    unnamed x4, local copies, waits for them, and re-layouts  3.22 us

profile of v3, /device:TPU:0, one launch (start us, length us, event | category | flops | bytes accessed | tf_op | source)
XLA Modules:
  0.0 55.2 jit_solution(10620132170641917743)
XLA Ops:
  0.6 51.4 %shard_map.77 = (f32[1536,256]{1,0:T(8,128)}, f32[1,256]{1,0:T(1,128)}) custom-call(bf16[1536,256]{1,0:T(8,128)(2,1)} %it_h.1, bf16[1536,256]{1,0:T(8,128)(2,1)} %r_h.1, bf16[1536,384]{1,0:T(8,128)(2,1)} %leaf_h.1, bf16[5,1536,128]{2,1,0:T(8,128)(2,1)} %v_h.1, bf16[5,1536,128]{2,1,0:T(8,128)(2,1)} %u_h.1, f32[1,256]{1,0:T(1,128)} %bitcast.3), custom_call_target="tpu_custom_call" | custom-call | tf_op jit(solution)/shard_map/pallas_call | solution.py:237
  52.0 0.0 copy-start
  52.0 2.7 %copy.10 = f32[1536,256]{1,0:T(8,128)} copy(f32[1536,256]{1,0:T(8,128)} %get-tuple-element.8) | data formatting | bytes 3145728
  54.7 0.0 copy-done
  54.7 0.6 %copy.11 = f32[256]{0:T(256)} copy(f32[256]{0:T(256)S(1)} %bitcast.2) | data formatting | bytes 2048
Async XLA Ops:
  52.0 2.7 %copy-start = (f32[1,256]{1,0:T(1,128)S(1)}, f32[1,256]{1,0:T(1,128)}, u32[]{:S(2)}) copy-start(f32[1,256]{1,0:T(1,128)} %get-tuple-element.5) | copy-start | bytes 3076
